TPU v7x, 32 devices: a whole 2x2x4 slice. The times are simulated.
32 devices in a mesh: row: 8 (over y, x, core), col: 4 (over z).
Axes of the slice: x: 2, y: 2, z: 4, core: 2. Of those that a mesh axis runs over, the one named last changes fastest.
Arguments:
- descriptors: bfloat16 [32, 6144], P(None, ('row', 'col')), may hold values from -6 to 6
- densities: float32 [6144], P(('row', 'col')), may hold values from 0.25 to 4
- vectors: float32 [32, 6144], P(None, ('row', 'col')), may hold values from -6 to 6
Outputs:
- next_block: float32 [32, 6144], P(None, ('row', 'col'))
All inputs are finite; a program needn't handle non-finite values.
Results may differ from a plain program's by a relative error of at most 0.0036.
Values may be sent and summed in bfloat16 or wider, within the bound.
No kernel may reach another device: no remote copies, remote signals or barrier semaphores. Data moves between devices by JAX's collectives and lax.ppermute only.
A program may use at most 64 MiB of HBM per device.

v0:
```python
import math
import jax
import jax.numpy as jnp
from jax import lax
from jax.sharding import PartitionSpec as P

kernel_width = 8.0


def tile_terms(targets, target_norm, piece):
    piece_feat, piece_vals, piece_inv = piece
    piece_norm = jnp.sum(jnp.square(piece_feat.astype(jnp.float32)), axis=0)
    feature_dim, target_count = targets.shape
    span_rows = math.gcd(target_count, 512)
    block_count = target_count // span_rows
    blocks = targets.reshape(feature_dim, block_count, span_rows).transpose(1, 0, 2)
    norm_blocks = target_norm.reshape(block_count, span_rows)

    def tile_block(block_item):
        block_feat, block_norm = block_item
        inner_prod = lax.dot_general(
            block_feat, piece_feat, (((0,), (0,)), ((), ())), preferred_element_type=jnp.float32
        )
        kernel = jnp.exp(
            -(block_norm[:, None] + piece_norm[None, :] - 2.0 * inner_prod) / kernel_width
        ).astype(jnp.bfloat16)
        numerator = lax.dot_general(
            piece_vals, kernel, (((1,), (1,)), ((), ())), preferred_element_type=jnp.float32
        )
        degree = lax.dot_general(
            piece_inv, kernel, (((1,), (1,)), ((), ())), preferred_element_type=jnp.float32
        )
        return (numerator, degree)

    numerator, degree = lax.map(tile_block, (blocks, norm_blocks))
    numerator = numerator.transpose(1, 0, 2).reshape(piece_vals.shape[0], target_count)
    degree = degree.transpose(1, 0, 2).reshape(1, target_count)
    return (numerator, degree)


def accumulate(targets, vec_count):
    target_norm = jnp.sum(jnp.square(targets.astype(jnp.float32)), axis=0)

    def fold_piece(running, piece, start):
        numerator, degree = tile_terms(targets, target_norm, piece)
        return (numerator, degree)

    initial = (
        jnp.zeros((vec_count, targets.shape[1]), jnp.float32),
        jnp.zeros((1, targets.shape[1]), jnp.float32),
    )
    return (fold_piece, initial)


def per_device(descriptors, densities, vectors):
    highest = lax.Precision.HIGHEST
    vec_count = vectors.shape[0]
    weighted = (vectors / densities[None, :]).astype(jnp.bfloat16)
    inverse = (1.0 / densities).astype(jnp.bfloat16)[None, :]
    targets = lax.all_gather(descriptors, "col", axis=1, tiled=True)
    fold_piece, initial = accumulate(targets, vec_count)
    partial_value = fold_piece(
        initial,
        (
            lax.all_gather(descriptors, "row", axis=1, tiled=True),
            lax.all_gather(weighted, "row", axis=1, tiled=True),
            lax.all_gather(inverse, "row", axis=1, tiled=True),
        ),
        jnp.int32(0),
    )
    numerator, degree = (
        lax.psum_scatter(partial_value[0], "col", scatter_dimension=1, tiled=True),
        lax.psum_scatter(partial_value[1], "col", scatter_dimension=1, tiled=True),
    )
    diffused = numerator / degree
    samples_float = float(descriptors.shape[1] * lax.axis_size("row") * lax.axis_size("col"))
    coupling, diffused_gram, basis_gram = lax.psum(
        (
            jnp.dot(vectors, diffused.T, precision=highest),
            jnp.dot(diffused, diffused.T, precision=highest),
            jnp.dot(vectors, vectors.T, precision=highest),
        ),
        ("row", "col"),
    )
    remainder = diffused - jnp.dot(coupling.T, vectors, precision=highest) / samples_float
    cross_term = jnp.dot(coupling.T, coupling, precision=highest)
    basis_term = jnp.dot(
        coupling.T, jnp.dot(basis_gram, coupling, precision=highest), precision=highest
    )
    spread = (
        diffused_gram
        - 2.0 * cross_term / samples_float
        + basis_term / (samples_float * samples_float)
    )
    factor = jnp.linalg.cholesky(spread)
    solved = jax.scipy.linalg.solve_triangular(factor, remainder, lower=True)
    return math.sqrt(samples_float) * solved


def solution(mesh):
    return jax.shard_map(
        per_device,
        mesh=mesh,
        in_specs=(P(None, ("row", "col")), P(("row", "col")), P(None, ("row", "col"))),
        out_specs=P(None, ("row", "col")),
        check_vma=False,
    )
```

profile of v0, /device:TPU:0, one launch (start us, length us, event | category | flops | bytes accessed | tf_op | source)
XLA Modules:
  0.0 157.3 jit_solution(3891402411580507994)
XLA Ops:
  6.5 11.0 %all-gather.2 = bf16[8,192,32]{1,2,0:T(8,128)(2,1)S(1)} all-gather(bf16[1,192,32]{1,2,0:T(8,128)(2,1)} %bitcast.102), channel_id=1, replica_groups=mesh['row'=8,'col'=4] {'row'}, dimensions={0}, use_global_device_ids=true | all-gather | bytes 110592 | tf_op jit(solution)/shard_map/all_gather | solution.py:65
  17.5 13.6 %all-gather.1 = bf16[4,192,32]{1,2,0:T(8,128)(2,1)S(1)} all-gather(bf16[1,192,32]{1,2,0:T(8,128)(2,1)} %bitcast.103), channel_id=1, replica_groups=mesh['row'=8,'col'=4] {'col'}, dimensions={0}, use_global_device_ids=true | all-gather | bytes 61440 | tf_op jit(solution)/shard_map/all_gather | solution.py:60
  31.7 9.0 %all-gather.3 = bf16[8,192,32]{1,2,0:T(8,128)(2,1)S(1)} all-gather(bf16[1,192,32]{1,2,0:T(8,128)(2,1)S(1)} %fusion.17), channel_id=1, replica_groups=mesh['row'=8,'col'=4] {'row'}, dimensions={0}, use_global_device_ids=true | all-gather | bytes 110592 | tf_op jit(solution)/shard_map/all_gather | solution.py:66
  40.9 0.6 dynamic-slice
  42.2 0.2 dynamic-update-slice.3
  42.4 13.2 %all-reduce = bf16[1536]{0:T(1024)(128)(2,1)S(1)} all-reduce(bf16[1536]{0:T(1024)(128)(2,1)S(1)} %dynamic-update-slice.3), channel_id=2, replica_groups=mesh['row'=8,'col'=4] {'row'}, use_global_device_ids=true, to_apply=%add | all-reduce | flops 1536 | bytes 6144
  55.6 3.6 %while.12 = (s32[]{:T(128)}, f32[3,32,256]{2,1,0:T(8,128)S(1)}, f32[3,1,256]{2,1,0:T(1,128)S(1)}, f32[3,256]{1,0:T(4,128)S(1)}, f32[1536]{0:T(1024)S(1)}, /*inde...) while((s32[]{:T(128)}, f32[3,32,256]{2,1,0:T(8,128)S(1)}, ...), condition=%wide.region_3.4_spmd, body=%wide.region_2.3_spmd.sunk | while | flops 53477376 | bytes 2623605 | solution.py:35
  55.7 0.5 fusion.52
  56.2 0.3 fusion.53
  56.5 0.3 fusion.54
  56.8 0.6 fusion.52
  57.4 0.3 fusion.53
  57.7 0.3 fusion.54
  58.0 0.6 fusion.52
  58.6 0.3 fusion.53
  58.9 0.3 fusion.54
  59.2 1.0 copy.40
  60.3 0.9 copy.42
  61.2 0.2 fusion.19
  61.4 19.1 %reduce-scatter.9.cloned.1.call-done = f32[192,1]{1,0:T(8,128)} async-done(((f32[768,1]{1,0:T(8,128)}), f32[192,1]{1,0:T(8,128)}) %reduce-scatter.9.cloned.1.call-update) | async-done | bytes 784
  80.4 1.0 copy.41
  81.4 20.4 %reduce-scatter.7.cloned.1.call-done = f32[192,32]{1,0:T(8,128)} async-done(((f32[768,32]{1,0:T(8,128)}), f32[192,32]{1,0:T(8,128)}) %reduce-scatter.7.cloned.1.call-update) | async-done | bytes 24592
  101.8 1.0 copy.39
  102.8 0.2 fusion.18
  103.0 0.2 convolution_bitcast_fusion.2
  103.1 39.0 %all-reduce.1 = (f32[32,32]{0,1:T(8,128)S(1)}, f32[32,32]{0,1:T(8,128)S(1)}, f32[32,32]{1,0:T(8,128)S(1)}) all-reduce(f32[32,32]{0,1:T(8,128)S(1)} %convolution_bitcast_fusion.2, f32[32,32]{0,1:T(8,128)S(1)} %fusion.18, f32[32,32]{1,0:T(8,128)S(1)} %fusion.19), channel_id=1, replica_groups=mesh['row'=8,'col'=4] {'row','col'}, use_global_device_ids=true, to_apply=%region_7.8 | all-reduce | flops 3072 | bytes 24576 | tf_op jit(solution)/shard_map/psum | solution.py:77
  142.6 0.2 fusion.12
  142.9 2.9 %cholesky.16 = f32[32,32]{1,0:T(8,128)S(1)} custom-call(f32[32,32]{1,0:T(8,128)S(1)} %fusion.16), custom_call_target="Cholesky" | custom-call | tf_op jit(solution)/shard_map/jit(cholesky)/cholesky | solution.py:95
  145.8 0.6 compare_reduce_fusion
  146.5 0.7 fusion.14
  147.1 2.4 %custom-call.7 = f32[1,32,32]{1,2,0:T(8,128)S(1)} custom-call(f32[1,32,32]{2,1,0:T(8,128)S(1)} %fusion.14), custom_call_target="InvertDiagBlocksLowerTriangular" | custom-call | tf_op jit(solution)/shard_map/jit(_solve_triangular)/triangular_solve | solution.py:96
  149.6 0.9 convolution_multiply_fusion.1
  (36 shorter events, 1.4 us)
Async XLA Ops:
  6.5 25.1 %copy-start.1 = (f32[192]{0:T(256)S(1)}, f32[192]{0:T(256)}, u32[]{:S(2)}) copy-start(f32[192]{0:T(256)} %param.6) | copy-start | bytes 2308
  6.5 25.1 %copy-start = (f32[32,192]{1,0:T(8,128)S(1)}, f32[32,192]{1,0:T(8,128)}, u32[]{:S(2)}) copy-start(f32[32,192]{1,0:T(8,128)} %param.7) | copy-start | bytes 73732
  6.5 73.9 %reduce-scatter.9.cloned.1.call-start = ((), (), s32[]{:S(2)}) async-start(), calls=%async_computation.3 | async-start | bytes 491520
  31.2 9.8 %copy-start.2 = (u32[32]{0:T(128)S(1)}, u32[32]{0:T(128)}, u32[]{:S(2)}) copy-start(u32[32]{0:T(128)} %constant.83) | copy-start | bytes 388
  60.2 41.6 %reduce-scatter.7.cloned.1.call-start = ((), (), s32[]{:S(2)}) async-start(), calls=%async_computation.2 | async-start | bytes 491520
Sparse Core Ops, SparseCore 0:
  60.3 20.0 reduce-scatter.8
  82.7 19.0 reduce-scatter.6
where the time goes:
time: 158 us; the launch traced here: 157 us
  blocking collectives  85.7 us (54%)
  waiting for transfers between devices  39.5 us (25%)
  between operations  14.2 us (9%)
  other arithmetic  6.76 us (4%)
  matrix products  5.55 us (4%)
  local copies, waits for them, and re-layouts  5.41 us (3%)
    unnamed x4, waiting for transfers between devices  39.5 us
    psum x1, blocking collectives, per_device(): lax.psum((jnp.dot(vectors, diffused.T, precision=highest), jnp.dot(diffus...  39 us
    all_gather x1, blocking collectives, per_device(): targets = lax.all_gather(descriptors, 'col', axis=1, tiled=True)  13.6 us
    unnamed x1, blocking collectives  13.2 us
    all_gather x1, blocking collectives, per_device(): lax.all_gather(descriptors, 'row', axis=1, tiled=True)  11 us
    all_gather x1, blocking collectives, per_device(): lax.all_gather(weighted, 'row', axis=1, tiled=True)  9.01 us
    unnamed x16, local copies, waits for them, and re-layouts  5.06 us
    another operation x3, other arithmetic, per_device(): factor = jnp.linalg.cholesky(spread)  3.6 us
  transfers between devices with their start and end apart: 2, of which 2 were waited for; matrix products, arithmetic and copies ran while one was open for 1% of the time, Pallas kernels for 0%

commit v1 on v0

--- a/solution.py
+++ b/solution.py
@@ -62,7 +62,7 @@
     partial_value = fold_piece(
         initial,
         (
-            lax.all_gather(descriptors, "row", axis=1, tiled=True),
+            jnp.concatenate(lax.all_gather(descriptors, "row"), axis=1),
             lax.all_gather(weighted, "row", axis=1, tiled=True),
             lax.all_gather(inverse, "row", axis=1, tiled=True),
         ),

time: 158 us -> 158 us (level)
    unnamed x16 -> x17, local copies, waits for them, and re-layouts: 5.06 us -> 4.92 us
where the time goes in v1:
time: 158 us; the launch traced here: 157 us
  blocking collectives  85.5 us (54%)
  waiting for transfers between devices  39.6 us (25%)
  between operations  14.3 us (9%)
  other arithmetic  6.81 us (4%)
  matrix products  5.55 us (4%)
  local copies, waits for them, and re-layouts  5.49 us (3%)
    unnamed x4, waiting for transfers between devices  39.6 us
    psum x1, blocking collectives, per_device(): lax.psum((jnp.dot(vectors, diffused.T, precision=highest), jnp.dot(diffus...  38.9 us
    all_gather x1, blocking collectives, per_device(): targets = lax.all_gather(descriptors, 'col', axis=1, tiled=True)  13.4 us
    unnamed x1, blocking collectives  13.2 us
    all_gather x1, blocking collectives, per_device(): lax.all_gather(descriptors, 'row')  11 us
    all_gather x1, blocking collectives, per_device(): lax.all_gather(weighted, 'row', axis=1, tiled=True)  9.01 us
    unnamed x17, local copies, waits for them, and re-layouts  4.92 us
    another operation x3, other arithmetic, per_device(): factor = jnp.linalg.cholesky(spread)  3.6 us
  transfers between devices with their start and end apart: 2, of which 2 were waited for; matrix products, arithmetic and copies ran while one was open for 1% of the time, Pallas kernels for 0%

profile of v1, /device:TPU:0, one launch (start us, length us, event | category | flops | bytes accessed | tf_op | source)
XLA Modules:
  0.0 157.2 jit_solution(876172886935195600)
XLA Ops:
  6.5 11.0 %all-gather = bf16[256,192]{1,0:T(8,128)(2,1)S(1)} all-gather(bf16[32,192]{1,0:T(8,128)(2,1)} %param.5), channel_id=2, replica_groups=mesh['row'=8,'col'=4] {'row'}, dimensions={0}, use_global_device_ids=true | all-gather | bytes 110592 | tf_op jit(solution)/shard_map/all_gather | solution.py:65
  17.9 13.4 %all-gather.2 = bf16[4,192,32]{1,2,0:T(8,128)(2,1)S(1)} all-gather(bf16[1,192,32]{1,2,0:T(8,128)(2,1)S(1)} %bitcast.106), channel_id=1, replica_groups=mesh['row'=8,'col'=4] {'col'}, dimensions={0}, use_global_device_ids=true | all-gather | bytes 61440 | tf_op jit(solution)/shard_map/all_gather | solution.py:60
  31.6 9.0 %all-gather.3 = bf16[8,192,32]{1,2,0:T(8,128)(2,1)S(1)} all-gather(bf16[1,192,32]{1,2,0:T(8,128)(2,1)S(1)} %fusion.17), channel_id=1, replica_groups=mesh['row'=8,'col'=4] {'row'}, dimensions={0}, use_global_device_ids=true | all-gather | bytes 110592 | tf_op jit(solution)/shard_map/all_gather | solution.py:66
  40.9 0.6 dynamic-slice
  42.1 0.2 dynamic-update-slice.3
  42.4 13.2 %all-reduce = bf16[1536]{0:T(1024)(128)(2,1)S(1)} all-reduce(bf16[1536]{0:T(1024)(128)(2,1)S(1)} %dynamic-update-slice.3), channel_id=3, replica_groups=mesh['row'=8,'col'=4] {'row'}, use_global_device_ids=true, to_apply=%add | all-reduce | flops 1536 | bytes 6144
  55.6 3.6 %while.12 = (s32[]{:T(128)}, f32[3,32,256]{2,1,0:T(8,128)S(1)}, f32[3,1,256]{2,1,0:T(1,128)S(1)}, f32[3,256]{1,0:T(4,128)S(1)}, f32[1536]{0:T(1024)S(1)}, /*inde...) while((s32[]{:T(128)}, f32[3,32,256]{2,1,0:T(8,128)S(1)}, ...), condition=%wide.region_3.4_spmd, body=%wide.region_2.3_spmd.sunk | while | flops 53477376 | bytes 2623605 | solution.py:35
  55.6 0.5 fusion.52
  56.1 0.3 fusion.53
  56.4 0.3 fusion.54
  56.8 0.6 fusion.52
  57.3 0.3 fusion.53
  57.6 0.3 fusion.54
  58.0 0.6 fusion.52
  58.5 0.3 fusion.53
  58.8 0.3 fusion.54
  59.2 1.0 copy.41
  60.2 0.9 copy.43
  61.2 0.2 fusion.19
  61.3 19.1 %reduce-scatter.9.cloned.1.call-done = f32[192,1]{1,0:T(8,128)} async-done(((f32[768,1]{1,0:T(8,128)}), f32[192,1]{1,0:T(8,128)}) %reduce-scatter.9.cloned.1.call-update) | async-done | bytes 784
  80.4 1.0 copy.42
  81.4 20.5 %reduce-scatter.7.cloned.1.call-done = f32[192,32]{1,0:T(8,128)} async-done(((f32[768,32]{1,0:T(8,128)}), f32[192,32]{1,0:T(8,128)}) %reduce-scatter.7.cloned.1.call-update) | async-done | bytes 24592
  101.8 1.0 copy.40
  102.8 0.2 fusion.18
  103.0 0.2 convolution_bitcast_fusion.2
  103.1 38.9 %all-reduce.1 = (f32[32,32]{0,1:T(8,128)S(1)}, f32[32,32]{0,1:T(8,128)S(1)}, f32[32,32]{1,0:T(8,128)S(1)}) all-reduce(f32[32,32]{0,1:T(8,128)S(1)} %convolution_bitcast_fusion.2, f32[32,32]{0,1:T(8,128)S(1)} %fusion.18, f32[32,32]{1,0:T(8,128)S(1)} %fusion.19), channel_id=1, replica_groups=mesh['row'=8,'col'=4] {'row','col'}, use_global_device_ids=true, to_apply=%region_7.8 | all-reduce | flops 3072 | bytes 24576 | tf_op jit(solution)/shard_map/psum | solution.py:77
  142.6 0.2 fusion.12
  142.8 2.9 %cholesky.16 = f32[32,32]{1,0:T(8,128)S(1)} custom-call(f32[32,32]{1,0:T(8,128)S(1)} %fusion.16), custom_call_target="Cholesky" | custom-call | tf_op jit(solution)/shard_map/jit(cholesky)/cholesky | solution.py:95
  145.8 0.6 compare_reduce_fusion
  146.4 0.7 fusion.14
  147.1 2.4 %custom-call.7 = f32[1,32,32]{1,2,0:T(8,128)S(1)} custom-call(f32[1,32,32]{2,1,0:T(8,128)S(1)} %fusion.14), custom_call_target="InvertDiagBlocksLowerTriangular" | custom-call | tf_op jit(solution)/shard_map/jit(_solve_triangular)/triangular_solve | solution.py:96
  149.5 0.9 convolution_multiply_fusion.1
  (39 shorter events, 1.5 us)
Async XLA Ops:
  6.5 11.4 %copy-start.1 = (bf16[32,192]{1,0:T(8,128)(2,1)S(1)}, bf16[32,192]{1,0:T(8,128)(2,1)}, u32[]{:S(2)}) copy-start(bf16[32,192]{1,0:T(8,128)(2,1)} %param.5) | copy-start | bytes 36868
  6.5 25.1 %copy-start.2 = (f32[192]{0:T(256)S(1)}, f32[192]{0:T(256)}, u32[]{:S(2)}) copy-start(f32[192]{0:T(256)} %param.6) | copy-start | bytes 2308
  6.5 25.1 %copy-start = (f32[32,192]{1,0:T(8,128)S(1)}, f32[32,192]{1,0:T(8,128)}, u32[]{:S(2)}) copy-start(f32[32,192]{1,0:T(8,128)} %param.7) | copy-start | bytes 73732
  6.5 73.8 %reduce-scatter.9.cloned.1.call-start = ((), (), s32[]{:S(2)}) async-start(), calls=%async_computation.3 | async-start | bytes 491520
  17.7 23.2 %copy-start.3 = (u32[32]{0:T(128)S(1)}, u32[32]{0:T(128)}, u32[]{:S(2)}) copy-start(u32[32]{0:T(128)} %constant.83) | copy-start | bytes 388
  60.2 41.6 %reduce-scatter.7.cloned.1.call-start = ((), (), s32[]{:S(2)}) async-start(), calls=%async_computation.2 | async-start | bytes 491520
Sparse Core Ops, SparseCore 0:
  60.3 20.0 reduce-scatter.8
  82.7 19.0 reduce-scatter.6
